TPU v7x, 512 devices: a whole 4x4x16 slice. The times are simulated.
512 devices in a mesh: dp: 8 (over x, core), expert: 64 (over z, y).
Axes of the slice: x: 4, y: 4, z: 16, core: 2. Of those that a mesh axis runs over, the one named last changes fastest.
Arguments:
- scores: int32 [64, 4096], P('expert', 'dp'), may hold values from 0 to 4095
- tokens: bfloat16 [4096, 4096], P('dp', 'expert'), may hold values from -6 to 6
- w_gate: bfloat16 [64, 1536, 4096], P('expert', 'dp'), may hold values from -0.09375 to 0.09375
- w_up: bfloat16 [64, 1536, 4096], P('expert', 'dp'), may hold values from -0.09375 to 0.09375
- w_down: bfloat16 [64, 1536, 4096], P('expert', 'dp'), may hold values from -0.15625 to 0.15625
Outputs:
- mixed: bfloat16 [4096, 4096], P('dp', 'expert')
Inputs may be any that keep to these rules, and one draw needn't show every extreme that they name: `scores`: score bins.
All inputs are finite; a program needn't handle non-finite values.
Results may differ from a plain program's by a relative error of at most 0.02.
Values may be sent and summed in bfloat16 or wider, within the bound.
A program may use at most 64 MiB of HBM per device.

v0:
```python
import jax
import jax.numpy as jnp
from jax import lax
from jax.sharding import PartitionSpec as P

CHOSEN = 4
LEVELS = 64
score_step = 1.0 / 512.0


def entering(value, axis, combine, identity):
    size, position = (lax.axis_size(axis), lax.axis_index(axis))
    everything = jax.tree.map(lambda part: lax.all_gather(part, axis), value)
    start = jax.tree.map(
        lambda part, zero: jnp.broadcast_to(jnp.asarray(zero, part.dtype), part.shape),
        value,
        identity,
    )

    def turn(k, before):
        reached = k < position
        new = combine(before, jax.tree.map(lambda part: part[k], everything))
        return jax.tree.map(lambda a, b: jnp.where(reached, a, b), new, before)

    return lax.fori_loop(0, size, turn, start)


def add_pair(earlier, later):
    return (earlier[0] + later[0], earlier[1] + later[1])


def project_rows(inputs, weight_rows):
    return lax.dot_general(
        inputs, weight_rows, (((1,), (1,)), ((), ())), preferred_element_type=jnp.float32
    )


def local(scores, tokens, w_gate, w_up, w_down):
    score_row = scores[0]
    tok_rows = score_row.shape[0]
    dp_size = lax.axis_size("dp")
    exp_size = lax.axis_size("expert")
    capacity = CHOSEN * tok_rows * dp_size // exp_size
    all_tokens = tok_rows * dp_size
    block = tokens.shape[1]
    first_tok = lax.axis_index("dp") * tok_rows
    bin_ids = jnp.arange(LEVELS, dtype=jnp.int32)
    coarse = score_row // LEVELS
    fine_bin = score_row % LEVELS
    local_coarse = jnp.sum(
        (coarse[:, None] == bin_ids[None, :]).astype(jnp.int32), axis=0, dtype=jnp.int32
    )
    coarse_counts = lax.psum(local_coarse, "dp")
    above_coarse = all_tokens - jnp.cumsum(coarse_counts, dtype=jnp.int32)
    cut_coarse = jnp.sum((above_coarse >= capacity).astype(jnp.int32), dtype=jnp.int32)
    need = capacity - jnp.sum(jnp.where(bin_ids == cut_coarse, above_coarse, 0), dtype=jnp.int32)
    inside = (coarse == cut_coarse)[:, None]
    local_fine = jnp.sum(
        ((fine_bin[:, None] == bin_ids[None, :]) & inside).astype(jnp.int32),
        axis=0,
        dtype=jnp.int32,
    )
    fine_counts = lax.psum(local_fine, "dp")
    above_fine = jnp.sum(fine_counts, dtype=jnp.int32) - jnp.cumsum(fine_counts, dtype=jnp.int32)
    cut_fine = jnp.sum((above_fine >= need).astype(jnp.int32), dtype=jnp.int32)
    allowed = need - jnp.sum(jnp.where(bin_ids == cut_fine, above_fine, 0), dtype=jnp.int32)
    cutoff = cut_coarse * LEVELS + cut_fine
    tie_mask = (score_row == cutoff).astype(jnp.int32)
    over_mask = (score_row > cutoff).astype(jnp.int32)
    tie_before, over_before = entering(
        (jnp.sum(tie_mask, dtype=jnp.int32), jnp.sum(over_mask, dtype=jnp.int32)),
        "dp",
        add_pair,
        (jnp.int32(0), jnp.int32(0)),
    )
    tie_rank = tie_before + jnp.cumsum(tie_mask, dtype=jnp.int32) - tie_mask
    chosen = (over_mask > 0) | (tie_mask > 0) & (tie_rank < allowed)
    chosen_int = chosen.astype(jnp.int32)
    slot_ids = (
        over_before
        + jnp.minimum(tie_before, allowed)
        + jnp.cumsum(chosen_int, dtype=jnp.int32)
        - chosen_int
    )
    weight = jnp.exp(score_row.astype(jnp.float32) * score_step)
    slot_dest = jnp.where(chosen, slot_ids, capacity)
    token_ids = (first_tok + jnp.arange(tok_rows, dtype=jnp.int32)).astype(jnp.float32)
    own_tables = jnp.zeros((2, capacity), jnp.float32)
    own_tables = own_tables.at[0, slot_dest].set(token_ids, mode="drop")
    own_tables = own_tables.at[1, slot_dest].set(weight, mode="drop")
    column = lax.psum(own_tables, "dp")
    table_data = lax.all_gather(column[None], "expert", axis=0, tiled=True)
    slot_tokens = table_data[:, 0, :].astype(jnp.int32)
    slot_weight = table_data[:, 1, :]
    gathered = lax.all_gather(tokens, "dp", axis=0, tiled=True)
    outgoing = gathered[slot_tokens]
    inputs = lax.all_to_all(outgoing, "expert", split_axis=0, concat_axis=2, tiled=True)[0]
    gate_val = project_rows(inputs, w_gate[0])
    up_val = project_rows(inputs, w_up[0])
    hidden = (jax.nn.silu(gate_val) * up_val).astype(jnp.bfloat16)
    computed = jnp.dot(hidden, w_down[0], preferred_element_type=jnp.float32).astype(jnp.bfloat16)[
        None
    ]
    returned = lax.all_to_all(computed, "expert", split_axis=2, concat_axis=0, tiled=True)
    term_rows = (
        jnp.zeros((all_tokens, block), jnp.float32)
        .at[slot_tokens.reshape(-1)]
        .add((returned.astype(jnp.float32) * slot_weight[:, :, None]).reshape(-1, block))
    )
    summed = lax.psum_scatter(
        term_rows.astype(jnp.bfloat16), "dp", scatter_dimension=0, tiled=True
    ).astype(jnp.float32)
    den_row = lax.psum(jnp.where(chosen, weight, jnp.float32(0.0)), "expert")
    return (summed / jnp.maximum(den_row, jnp.float32(1.0))[:, None]).astype(jnp.bfloat16)


def solution(mesh):
    in_specs = (
        P("expert", "dp"),
        P("dp", "expert"),
        P("expert", "dp", None),
        P("expert", "dp", None),
        P("expert", "dp", None),
    )
    out_specs = P("dp", "expert")
    return jax.shard_map(local, mesh=mesh, in_specs=in_specs, out_specs=out_specs, check_vma=False)
```

profile of v0, /device:TPU:8, one launch (start us, length us, event | category | flops | bytes accessed | tf_op | source)
XLA Modules:
  0.0 840.0 jit_solution(11131477647967400313)
XLA Ops:
  6.5 0.8 add_select_fusion
  7.5 9.2 %psum.28 = s32[64,1]{0,1:T(1,128)S(1)} all-reduce(s32[64,1]{0,1:T(1,128)S(1)} %bitcast.111), channel_id=1, replica_groups=mesh['dp'=8,'expert'=64] {'dp'}, use_global_device_ids=true, to_apply=%region_1.2 | all-reduce | flops 64 | bytes 512 | tf_op jit(solution)/shard_map/psum | solution.py:53
  17.0 0.7 fusion.31
  17.7 1.3 fusion.32
  20.5 7.3 psum.29
  27.7 0.7 reduce_sum.84
  29.3 0.7 subtract_reduce_fusion
  30.1 0.7 fusion.33
  30.8 1.4 fusion.34
  32.9 1.4 convert_reduce_fusion.3
  34.2 0.7 compare_reduce_fusion
  34.9 1.3 dynamic-slice
  36.2 1.3 dynamic-update-slice.1
  37.5 1.3 dynamic-update-slice
  39.4 8.9 %all-reduce.4 = (s32[8]{0:T(128)S(1)}, s32[8]{0:T(128)S(1)}) all-reduce(s32[8]{0:T(128)S(1)} %dynamic-update-slice, s32[8]{0:T(128)S(1)} %dynamic-update-slice.1), channel_id=1, replica_groups=mesh['dp'=8,'expert'=64] {'dp'}, use_global_device_ids=true, to_apply=%add.2 | all-reduce | flops 16 | bytes 128
  48.3 20.9 %while.15 = (s32[]{:T(128)}, s32[]{:T(128)}, s32[]{:T(128)}, s32[]{:T(128)}, s32[8]{0:T(128)S(1)}, /*index=5*/s32[8]{0:T(128)S(1)}, s32[]{:T(128)}) while((s32[]{:T(128)}, s32[]{:T(128)}, s32[]{:T(128)}, s32[]{:T(128)}, s32[8]{0:T(128)S(1)}, /*index=5*/s32[8]{0:T(128)S(1)}, s32[]{:T(128)}) %tuple.38), condition=%wide.region_13.14_spmd, body=%wide.region_12.13_spmd.sunk | while | flops 7 | bytes 168 | solution.py:25
  49.6 0.7 dynamic_slice.17
  52.2 0.7 dynamic_slice.17
  57.4 0.7 dynamic_slice.17
  60.1 0.7 dynamic_slice.17
  65.3 0.7 dynamic_slice.17
  67.9 0.7 dynamic_slice.17
  69.7 0.8 fusion.30
  71.1 0.7 or_select_fusion
  71.8 24.8 %scatter_fusion = f32[2,256]{1,0:T(2,128)S(1)} fusion(f32[2,256]{1,0:T(2,128)S(1)} %broadcast_in_dim.38, s32[512]{0:T(512)S(1)} %bitcast.91, f32[512]{0:T(512)S(1)} %add_convert_fusion), kind=kCustom, calls=%fused_computation.1 | custom fusion | bytes 10240 | tf_op jit(solution)/shard_map/scatter | solution.py:89
  96.6 24.8 %scatter_fusion.1 = f32[2,256]{1,0:T(2,128)S(1)} fusion(f32[2,256]{1,0:T(2,128)S(1)} %scatter_fusion, s32[512]{0:T(512)S(1)} %bitcast.90, f32[512]{0:T(512)S(1)} %get-tuple-element.141), kind=kCustom, calls=%fused_computation.2 | custom fusion | bytes 10240 | tf_op jit(solution)/shard_map/scatter | solution.py:90
  121.4 12.4 %psum.30 = f32[1,2,256]{2,1,0:T(2,128)S(1)} all-reduce(f32[1,2,256]{2,1,0:T(2,128)S(1)} %bitcast.89), channel_id=1, replica_groups=mesh['dp'=8,'expert'=64] {'dp'}, use_global_device_ids=true, to_apply=%region_21.22 | all-reduce | flops 512 | bytes 4096 | tf_op jit(solution)/shard_map/psum | solution.py:91
  133.8 106.1 %all_gather.22 = f32[64,2,256]{2,1,0:T(2,128)S(1)} all-gather(f32[1,2,256]{2,1,0:T(2,128)S(1)} %psum.30), channel_id=1, replica_groups=mesh['dp'=8,'expert'=64] {'expert'}, dimensions={0}, use_global_device_ids=true | all-gather | bytes 133120 | tf_op jit(solution)/shard_map/all_gather | solution.py:92
  240.2 13.9 %all_gather.23 = bf16[4096,64]{1,0:T(8,128)(2,1)S(1)} all-gather(bf16[512,64]{1,0:T(8,128)(2,1)S(1)} %copy.44), channel_id=1, replica_groups=mesh['dp'=8,'expert'=64] {'dp'}, dimensions={0}, use_global_device_ids=true | all-gather | bytes 589824 | tf_op jit(solution)/shard_map/all_gather | solution.py:95
  254.1 57.4 %gather_fusion = bf16[16384,64]{1,0:T(8,128)(2,1)} fusion(bf16[4096,64]{1,0:T(8,128)(2,1)S(1)} %all_gather.23, s32[16384]{0:T(1024)S(1)} %broadcast_clamp_fusion), kind=kCustom, calls=%fused_computation | custom fusion | bytes 4259840 | tf_op jit(solution)/shard_map/gather | solution.py:96
  311.5 4.8 copy.45
  316.2 111.0 %all_to_all.24 = bf16[64,256,64]{1,2,0:T(8,128)(2,1)S(1)} all-to-all(bf16[64,256,64]{1,2,0:T(8,128)(2,1)} %copy.45), channel_id=1, replica_groups=mesh['dp'=8,'expert'=64] {'expert'}, dimensions={0} | all-to-all | bytes 4194304 | tf_op jit(solution)/shard_map/all_to_all | solution.py:97
  427.3 1.3 copy-done.1
  429.2 0.8 copy-done.3
  430.0 5.0 fusion
  435.0 10.0 %copy.46 = bf16[1,256,4096]{1,0,2:T(2,128)(2,1)} copy(bf16[1,256,4096]{2,1,0:T(8,128)(2,1)} %fusion) | data formatting | bytes 4194304 | tf_op jit(solution)/shard_map/broadcast_in_dim | solution.py:101
  445.6 22.9 %reduce.10 = bf16[4096,256]{1,0:T(8,128)(2,1)} reduce(bf16[4096,1,256]{2,1,0:T(2,128)(2,1)} %bitcast.95, bf16[]{:T(256)} %broadcast.348), dimensions={1}, to_apply=%bitcast.74.reduce_sub_computation | reduce | bytes 4194306
  468.5 4.0 reshape.377
  472.4 6.1 all-to-all-start.1
  478.8 99.3 %all-to-all-done.1 = bf16[64,2,8192]{2,1,0:T(2,128)(2,1)} async-done(((bf16[64,2,8192]{2,1,0:T(2,128)(2,1)}), bf16[64,2,8192]{2,1,0:T(2,128)(2,1)}, u32[]{:S(2)}, u32[]{:S(2)}) %all-to-all-start.1) | async-done | bytes 2097184 | tf_op jit(solution)/shard_map/all_to_all | solution.py:104
  578.1 10.4 %reshape.378 = bf16[4096,1,256]{2,1,0:T(2,128)(2,1)} reshape(bf16[64,2,8192]{2,1,0:T(2,128)(2,1)} %all-to-all-done.1) | data formatting | bytes 4194304
  588.6 2.5 copy.47
  592.1 2.3 broadcast_multiply_fusion
  594.4 6.9 copy.49
  601.2 89.1 %scatter_custom_fusion.2 = f32[4096,64]{1,0:T(8,128)} fusion(s32[16384]{0:T(1024)S(1)} %bitcast.102, f32[16384,64]{1,0:T(8,128)} %copy.49, f32[]{:T(128)} %constant.75.clone.1), kind=kCustom, calls=%fused_computation.15 | custom fusion | flops 1048576 | bytes 1049088 | tf_op jit(solution)/shard_map/scatter-add | solution.py:108
  690.3 2.7 copy.50
  693.1 138.6 %psum.31 = f32[512]{0:T(512)S(1)} all-reduce(f32[512]{0:T(512)S(1)} %get-tuple-element.131), channel_id=1, replica_groups=mesh['dp'=8,'expert'=64] {'expert'}, use_global_device_ids=true, to_apply=%region_24.25 | all-reduce | flops 512 | bytes 4096 | tf_op jit(solution)/shard_map/psum | solution.py:113
  831.7 1.5 divide_convert_fusion
  (54 shorter events, 11.5 us)
Async XLA Ops:
  6.5 422.7 %copy-start = (bf16[1,192,4096]{2,1,0:T(8,128)(2,1)S(1)}, bf16[1,192,4096]{2,1,0:T(8,128)(2,1)}, u32[]{:S(2)}) copy-start(bf16[1,192,4096]{2,1,0:T(8,128)(2,1)} %param.11) | copy-start | bytes 4718596
  96.6 143.5 %copy-start.4 = (bf16[512,64]{0,1:T(8,128)(2,1)S(1)}, bf16[512,64]{0,1:T(8,128)(2,1)}, u32[]{:S(2)}) copy-start(bf16[512,64]{0,1:T(8,128)(2,1)} %param.8) | copy-start | bytes 196612
  316.2 112.4 %copy-start.2 = (bf16[1,192,4096]{2,1,0:T(8,128)(2,1)S(1)}, bf16[1,192,4096]{2,1,0:T(8,128)(2,1)}, u32[]{:S(2)}) copy-start(bf16[1,192,4096]{2,1,0:T(8,128)(2,1)} %param.9) | copy-start | bytes 4718596
  427.3 1.4 copy-start.1
  428.6 1.4 copy-start.3
  472.4 105.7 %all-to-all-start.1 = ((bf16[64,2,8192]{2,1,0:T(2,128)(2,1)}), bf16[64,2,8192]{2,1,0:T(2,128)(2,1)}, u32[]{:S(2)}, u32[]{:S(2)}) async-start(bf16[64,2,8192]{2,1,0:T(2,128)(2,1)} %reshape.377), calls=%async_computation.1 | async-start | bytes 4194304 | tf_op jit(solution)/shard_map/all_to_all | solution.py:104
  478.6 353.1 %reduce-scatter.2.cloned.1.call-start = ((), (), s32[]{:S(2)}) async-start(), calls=%async_computation.3 | async-start | bytes 589824 | tf_op jit(solution)/shard_map/reduce_scatter | solution.py:110
Sparse Core Ops, SparseCore 0:
  693.2 28.9 reduce-scatter.1
where the time goes:
time: 842 us; the launch traced here: 840 us
  blocking collectives  407 us (48%)
  local copies, waits for them, and re-layouts  166 us (20%)
  other arithmetic  128 us (15%)
  waiting for transfers between devices  99.3 us (12%)
  between operations  16.3 us (2%)
  loops' own time  10.4 us (1%)
    psum x1, blocking collectives, local(): den_row = lax.psum(jnp.where(chosen, weight, jnp.float32(0.0)), 'expert')  139 us
    all_to_all x1, blocking collectives, local(): lax.all_to_all(outgoing, 'expert', split_axis=0, concat_axis=2, tiled=True)  111 us
    all_gather x1, blocking collectives, local(): table_data = lax.all_gather(column[None], 'expert', axis=0, tiled=True)  106 us
    all_to_all x1, waiting for transfers between devices, local(): lax.all_to_all(computed, 'expert', split_axis=2, concat_axis=0, tiled=True)  99.3 us
    scatter-add x1, other arithmetic, local(): term_rows = jnp.zeros((all_tokens, block), jnp.float32).at[slot_tokens.re...  89.1 us
    gather x2, local copies, waits for them, and re-layouts, local(): outgoing = gathered[slot_tokens]  62.2 us
    scatter x1, local copies, waits for them, and re-layouts, local(): own_tables = own_tables.at[0, slot_dest].set(token_ids, mode='drop')  24.8 us
    scatter x1, local copies, waits for them, and re-layouts, local(): own_tables = own_tables.at[1, slot_dest].set(weight, mode='drop')  24.8 us
  transfers between devices with their start and end apart: 2, of which 1 were waited for; matrix products, arithmetic and copies ran while one was open for 0% of the time, Pallas kernels for 0%

commit v1 on v0

--- a/solution.py
+++ b/solution.py
@@ -89,7 +89,9 @@
     own_tables = own_tables.at[0, slot_dest].set(token_ids, mode="drop")
     own_tables = own_tables.at[1, slot_dest].set(weight, mode="drop")
     column = lax.psum(own_tables, "dp")
-    table_data = lax.all_gather(column[None], "expert", axis=0, tiled=True)
+    table_data = jnp.concatenate(
+        lax.all_to_all(jnp.stack([column[None]] * lax.axis_size("expert")), "expert", 0, 0), axis=0
+    )
     slot_tokens = table_data[:, 0, :].astype(jnp.int32)
     slot_weight = table_data[:, 1, :]
     gathered = lax.all_gather(tokens, "dp", axis=0, tiled=True)

time: 842 us -> 760 us (0.903)
  blocking collectives: 407 us -> 303 us
  starting transfers between devices: 6.18 us -> 24.9 us
    all_gather x1 -> x0, blocking collectives: 106 us -> none  [local(): table_data = lax.all_gather(column[None], 'expert', axis=0, tiled=True)]
    all_to_all x0 -> x1, starting transfers between devices: none -> 18.7 us  [local(): lax.all_to_all(jnp.stack([column[None]] * lax.axis_size('expert')), 'expe...]
  transfers between devices with their start and end apart: 2 -> 3, of which waited for: 1 -> 2; matrix products, arithmetic and copies ran while one was open for 0% -> 0% of each run, Pallas kernels for 0% -> 0%
where the time goes in v1:
time: 760 us; the launch traced here: 758 us
  blocking collectives  303 us (40%)
  local copies, waits for them, and re-layouts  167 us (22%)
  other arithmetic  128 us (17%)
  waiting for transfers between devices  102 us (13%)
  starting transfers between devices  24.9 us (3%)
  between operations  16.3 us (2%)
  loops' own time  10.4 us (1%)
    psum x1, blocking collectives, local(): den_row = lax.psum(jnp.where(chosen, weight, jnp.float32(0.0)), 'expert')  139 us
    all_to_all x1, blocking collectives, local(): lax.all_to_all(outgoing, 'expert', split_axis=0, concat_axis=2, tiled=True)  113 us
    all_to_all x1, waiting for transfers between devices, local(): lax.all_to_all(computed, 'expert', split_axis=2, concat_axis=0, tiled=True)  99.3 us
    scatter-add x1, other arithmetic, local(): term_rows = jnp.zeros((all_tokens, block), jnp.float32).at[slot_tokens.re...  89.1 us
    gather x2, local copies, waits for them, and re-layouts, local(): outgoing = gathered[slot_tokens]  62.2 us
    scatter x1, local copies, waits for them, and re-layouts, local(): own_tables = own_tables.at[0, slot_dest].set(token_ids, mode='drop')  24.8 us
    scatter x1, local copies, waits for them, and re-layouts, local(): own_tables = own_tables.at[1, slot_dest].set(weight, mode='drop')  24.8 us
    unnamed x2, other arithmetic  23.5 us
  transfers between devices with their start and end apart: 3, of which 2 were waited for; matrix products, arithmetic and copies ran while one was open for 0% of the time, Pallas kernels for 0%

profile of v1, /device:TPU:8, one launch (start us, length us, event | category | flops | bytes accessed | tf_op | source)
XLA Modules:
  0.0 758.1 jit_solution(15596121218694810841)
XLA Ops:
  6.5 0.8 add_select_fusion
  7.5 9.2 %psum.28 = s32[64,1]{0,1:T(1,128)S(1)} all-reduce(s32[64,1]{0,1:T(1,128)S(1)} %bitcast.112), channel_id=1, replica_groups=mesh['dp'=8,'expert'=64] {'dp'}, use_global_device_ids=true, to_apply=%region_1.2 | all-reduce | flops 64 | bytes 512 | tf_op jit(solution)/shard_map/psum | solution.py:53
  17.0 0.7 fusion.31
  17.7 1.3 fusion.32
  20.5 7.3 psum.29
  27.7 0.7 reduce_sum.84
  29.3 0.7 subtract_reduce_fusion
  30.1 0.7 fusion.33
  30.8 1.4 fusion.34
  32.9 1.4 convert_reduce_fusion.3
  34.2 0.7 compare_reduce_fusion
  34.9 1.3 dynamic-slice
  36.2 1.3 dynamic-update-slice.1
  37.5 1.3 dynamic-update-slice
  39.4 8.9 %all-reduce.4 = (s32[8]{0:T(128)S(1)}, s32[8]{0:T(128)S(1)}) all-reduce(s32[8]{0:T(128)S(1)} %dynamic-update-slice, s32[8]{0:T(128)S(1)} %dynamic-update-slice.1), channel_id=1, replica_groups=mesh['dp'=8,'expert'=64] {'dp'}, use_global_device_ids=true, to_apply=%add.2 | all-reduce | flops 16 | bytes 128
  48.3 20.9 %while.15 = (s32[]{:T(128)}, s32[]{:T(128)}, s32[]{:T(128)}, s32[]{:T(128)}, s32[8]{0:T(128)S(1)}, /*index=5*/s32[8]{0:T(128)S(1)}, s32[]{:T(128)}) while((s32[]{:T(128)}, s32[]{:T(128)}, s32[]{:T(128)}, s32[]{:T(128)}, s32[8]{0:T(128)S(1)}, /*index=5*/s32[8]{0:T(128)S(1)}, s32[]{:T(128)}) %tuple.38), condition=%wide.region_13.14_spmd, body=%wide.region_12.13_spmd.sunk | while | flops 7 | bytes 168 | solution.py:25
  52.2 0.7 dynamic_slice.17
  57.4 0.7 dynamic_slice.17
  60.1 0.7 dynamic_slice.17
  65.3 0.7 dynamic_slice.17
  69.7 0.8 fusion.30
  71.1 0.7 or_select_fusion
  71.8 24.8 %scatter_fusion = f32[2,256]{1,0:T(2,128)S(1)} fusion(f32[2,256]{1,0:T(2,128)S(1)} %broadcast_in_dim.20, s32[512]{0:T(512)S(1)} %bitcast.90, f32[512]{0:T(512)S(1)} %add_convert_fusion), kind=kCustom, calls=%fused_computation.1 | custom fusion | bytes 10240 | tf_op jit(solution)/shard_map/scatter | solution.py:89
  96.6 24.8 %scatter_fusion.1 = f32[2,256]{1,0:T(2,128)S(1)} fusion(f32[2,256]{1,0:T(2,128)S(1)} %scatter_fusion, s32[512]{0:T(512)S(1)} %bitcast.89, f32[512]{0:T(512)S(1)} %get-tuple-element.141), kind=kCustom, calls=%fused_computation.2 | custom fusion | bytes 10240 | tf_op jit(solution)/shard_map/scatter | solution.py:90
  121.4 12.4 %psum.30 = f32[2,256]{1,0:T(2,128)S(1)} all-reduce(f32[2,256]{1,0:T(2,128)S(1)} %scatter_fusion.1), channel_id=1, replica_groups=mesh['dp'=8,'expert'=64] {'dp'}, use_global_device_ids=true, to_apply=%region_21.22 | all-reduce | flops 512 | bytes 4096 | tf_op jit(solution)/shard_map/psum | solution.py:91
  133.8 0.7 stack.3
  134.5 18.7 %all-to-all-start = ((f32[64,1,2,256]{3,2,1,0:T(2,128)}), f32[64,1,2,256]{3,2,1,0:T(2,128)S(1)}, u32[]{:S(2)}, u32[]{:S(2)}) async-start(f32[64,1,2,256]{3,2,1,0:T(2,128)} %stack.3), calls=%async_computation | async-start | bytes 262144 | tf_op jit(solution)/shard_map/all_to_all | solution.py:93
  153.4 13.8 %all_gather.19 = bf16[4096,64]{1,0:T(8,128)(2,1)S(1)} all-gather(bf16[512,64]{1,0:T(8,128)(2,1)S(1)} %copy.44), channel_id=1, replica_groups=mesh['dp'=8,'expert'=64] {'dp'}, dimensions={0}, use_global_device_ids=true | all-gather | bytes 589824 | tf_op jit(solution)/shard_map/all_gather | solution.py:97
  167.2 2.6 all-to-all-done
  170.0 57.4 %gather_fusion = bf16[16384,64]{1,0:T(8,128)(2,1)} fusion(bf16[4096,64]{1,0:T(8,128)(2,1)S(1)} %all_gather.19, s32[16384]{0:T(1024)S(1)} %broadcast_clamp_fusion), kind=kCustom, calls=%fused_computation | custom fusion | bytes 4259840 | tf_op jit(solution)/shard_map/gather | solution.py:98
  227.4 4.8 copy.45
  232.2 113.2 %all_to_all.29 = bf16[64,256,64]{1,2,0:T(8,128)(2,1)S(1)} all-to-all(bf16[64,256,64]{1,2,0:T(8,128)(2,1)} %copy.45), channel_id=1, replica_groups=mesh['dp'=8,'expert'=64] {'expert'}, dimensions={0} | all-to-all | bytes 4194304 | tf_op jit(solution)/shard_map/all_to_all | solution.py:99
  345.4 1.3 copy-done.1
  347.3 0.8 copy-done.3
  348.1 5.0 fusion
  353.1 10.0 %copy.46 = bf16[1,256,4096]{1,0,2:T(2,128)(2,1)} copy(bf16[1,256,4096]{2,1,0:T(8,128)(2,1)} %fusion) | data formatting | bytes 4194304 | tf_op jit(solution)/shard_map/broadcast_in_dim | solution.py:103
  363.7 22.9 %reduce.10 = bf16[4096,256]{1,0:T(8,128)(2,1)} reduce(bf16[4096,1,256]{2,1,0:T(2,128)(2,1)} %bitcast.94, bf16[]{:T(256)} %broadcast.350), dimensions={1}, to_apply=%bitcast.74.reduce_sub_computation | reduce | bytes 4194306
  386.6 4.0 reshape.383
  390.5 6.1 all-to-all-start.2
  396.9 99.3 %all-to-all-done.2 = bf16[64,2,8192]{2,1,0:T(2,128)(2,1)} async-done(((bf16[64,2,8192]{2,1,0:T(2,128)(2,1)}), bf16[64,2,8192]{2,1,0:T(2,128)(2,1)}, u32[]{:S(2)}, u32[]{:S(2)}) %all-to-all-start.2) | async-done | bytes 2097184 | tf_op jit(solution)/shard_map/all_to_all | solution.py:106
  496.2 10.4 %reshape.384 = bf16[4096,1,256]{2,1,0:T(2,128)(2,1)} reshape(bf16[64,2,8192]{2,1,0:T(2,128)(2,1)} %all-to-all-done.2) | data formatting | bytes 4194304
  506.7 2.5 copy.47
  510.1 2.3 broadcast_multiply_fusion
  512.5 6.9 copy.49
  519.3 89.1 %scatter_custom_fusion.2 = f32[4096,64]{1,0:T(8,128)} fusion(s32[16384]{0:T(1024)S(1)} %bitcast.103, f32[16384,64]{1,0:T(8,128)} %copy.49, f32[]{:T(128)} %constant.75.clone.1), kind=kCustom, calls=%fused_computation.15 | custom fusion | flops 1048576 | bytes 1049088 | tf_op jit(solution)/shard_map/scatter-add | solution.py:110
  608.4 2.7 copy.50
  611.2 138.6 %psum.31 = f32[512]{0:T(512)S(1)} all-reduce(f32[512]{0:T(512)S(1)} %get-tuple-element.131), channel_id=1, replica_groups=mesh['dp'=8,'expert'=64] {'expert'}, use_global_device_ids=true, to_apply=%region_24.25 | all-reduce | flops 512 | bytes 4096 | tf_op jit(solution)/shard_map/psum | solution.py:115
  749.8 1.5 divide_convert_fusion
  (56 shorter events, 12.8 us)
Async XLA Ops:
  6.5 340.8 %copy-start = (bf16[1,192,4096]{2,1,0:T(8,128)(2,1)S(1)}, bf16[1,192,4096]{2,1,0:T(8,128)(2,1)}, u32[]{:S(2)}) copy-start(bf16[1,192,4096]{2,1,0:T(8,128)(2,1)} %param.11) | copy-start | bytes 4718596
  96.6 56.6 %copy-start.4 = (bf16[512,64]{0,1:T(8,128)(2,1)S(1)}, bf16[512,64]{0,1:T(8,128)(2,1)}, u32[]{:S(2)}) copy-start(bf16[512,64]{0,1:T(8,128)(2,1)} %param.8) | copy-start | bytes 196612
  134.5 35.4 %all-to-all-start = ((f32[64,1,2,256]{3,2,1,0:T(2,128)}), f32[64,1,2,256]{3,2,1,0:T(2,128)S(1)}, u32[]{:S(2)}, u32[]{:S(2)}) async-start(f32[64,1,2,256]{3,2,1,0:T(2,128)} %stack.3), calls=%async_computation | async-start | bytes 262144 | tf_op jit(solution)/shard_map/all_to_all | solution.py:93
  232.2 114.6 %copy-start.2 = (bf16[1,192,4096]{2,1,0:T(8,128)(2,1)S(1)}, bf16[1,192,4096]{2,1,0:T(8,128)(2,1)}, u32[]{:S(2)}) copy-start(bf16[1,192,4096]{2,1,0:T(8,128)(2,1)} %param.9) | copy-start | bytes 4718596
  345.4 1.4 copy-start.1
  346.7 1.4 copy-start.3
  390.5 105.7 %all-to-all-start.2 = ((bf16[64,2,8192]{2,1,0:T(2,128)(2,1)}), bf16[64,2,8192]{2,1,0:T(2,128)(2,1)}, u32[]{:S(2)}, u32[]{:S(2)}) async-start(bf16[64,2,8192]{2,1,0:T(2,128)(2,1)} %reshape.383), calls=%async_computation.2 | async-start | bytes 4194304 | tf_op jit(solution)/shard_map/all_to_all | solution.py:106
  396.7 353.1 %reduce-scatter.2.cloned.1.call-start = ((), (), s32[]{:S(2)}) async-start(), calls=%async_computation.4 | async-start | bytes 589824 | tf_op jit(solution)/shard_map/reduce_scatter | solution.py:112
Sparse Core Ops, SparseCore 0:
  611.3 29.0 reduce-scatter.1
